TPU v7x, 32 devices: a whole 2x2x4 slice. The times are simulated.
32 devices in a mesh: rows: 4 (over x, core), slopes: 8 (over z, y).
Axes of the slice: x: 2, y: 2, z: 4, core: 2. Of those that a mesh axis runs over, the one named last changes fastest.
Arguments:
- reconstructor: bfloat16 [5120, 90112], P('rows', 'slopes'), may hold values from -0.375 to 0.375
- cov_slab: bfloat16 [90112, 256], P('slopes', 'rows'), may hold values from -0.4375 to 0.4375
- residual_in: float32 [5120, 5120], P('rows', 'slopes'), may hold values from -6 to 6
- propagation: bfloat16 [5120, 5120], P('rows', 'slopes'), may hold values from -0.078125 to 0.078125
Outputs:
- residual_out: float32 [5120, 5120], P('rows', 'slopes')
- projected: float32 [5120, 5120], P('rows', 'slopes')
All inputs are finite; a program needn't handle non-finite values.
Results may differ from a plain program's by a relative error of at most 0.0046.
Values may be sent and summed in bfloat16 or wider, within the bound.
No kernel may reach another device: no remote copies, remote signals or barrier semaphores. Data moves between devices by JAX's collectives and lax.ppermute only.
A program may use at most 128 MiB of HBM per device.

v0:
```python
import jax
import jax.numpy as jnp
from jax import lax
from jax.sharding import PartitionSpec as P

SLOPES = 90112
SLAB = 256


def spread(x, axis, root):
    mine = lax.axis_index(axis) == root
    return lax.psum(jnp.where(mine, x, jnp.zeros_like(x)), axis)


def body(reconstructor, cov_slab, residual_in, propagation):
    row_index = lax.axis_index("rows")
    slope_index = lax.axis_index("slopes")
    row_block = propagation.shape[0]
    col_block = propagation.shape[1]
    stride = SLOPES // SLAB
    picked_local = reconstructor[:, ::stride]
    d_rows, picked_rows = (
        lax.all_gather(propagation, "slopes", axis=1, tiled=True),
        lax.all_gather(picked_local, "slopes", axis=1, tiled=True),
    )
    partial_sum = jnp.dot(
        reconstructor,
        lax.all_gather(cov_slab, "rows", axis=1, tiled=True),
        preferred_element_type=jnp.float32,
    )
    reach = lax.psum(partial_sum, "slopes").astype(jnp.bfloat16)
    owner = slope_index * col_block // row_block
    offset = jnp.clip(slope_index * col_block - row_index * row_block, 0, row_block - col_block)
    d_local = lax.dynamic_slice_in_dim(d_rows, offset, col_block, 0)
    p_local = lax.dynamic_slice_in_dim(picked_rows, offset, col_block, 0)
    d_block, p_block = (spread(d_local, "rows", owner), spread(p_local, "rows", owner))
    update = lax.dot_general(
        reach, p_block, (((1,), (1,)), ((), ())), preferred_element_type=jnp.float32
    )
    residual_out = residual_in + update
    resid_low = residual_out.astype(jnp.bfloat16)
    columns = d_rows
    front = jnp.dot(
        columns,
        lax.all_gather(resid_low, "rows", axis=0, tiled=True),
        preferred_element_type=jnp.float32,
    ).astype(jnp.bfloat16)
    columns = d_block
    projected = lax.dot_general(
        lax.all_gather(front, "slopes", axis=1, tiled=True),
        columns,
        (((1,), (1,)), ((), ())),
        preferred_element_type=jnp.float32,
    )
    return (residual_out, projected)


def solution(mesh):
    placed = (P("rows", "slopes"), P("slopes", "rows"), P("rows", "slopes"), P("rows", "slopes"))
    return jax.shard_map(
        body,
        mesh=mesh,
        in_specs=placed,
        out_specs=(P("rows", "slopes"), P("rows", "slopes")),
        check_vma=False,
    )
```

profile of v0, /device:TPU:0, one launch (start us, length us, event | category | flops | bytes accessed | tf_op | source)
XLA Modules:
  0.0 648.7 jit_solution(1992956967964907286)
XLA Ops:
  7.2 0.0 all-gather.9.cloned.1.call-start
  7.2 0.7 all-gather.9.cloned.1.call-update
  7.9 0.0 all-gather.5.cloned.1.call-start
  7.9 0.7 all-gather.5.cloned.1.call-update
  8.6 0.0 all-reduce.4.cloned.1.call-start
  8.7 10.7 %slice.3 = bf16[1280,32]{1,0:T(8,128)(2,1)S(1)} slice(bf16[1280,11264]{1,0:T(8,128)(2,1)} %param.4), slice={[0:1280:1], [0:11264:352]} | slice | bytes 163840 | tf_op jit(solution)/shard_map/slice | solution.py:21
  19.5 0.2 copy.7
  19.6 36.3 %all_gather.16 = bf16[1280,256]{0,1:T(8,128)(2,1)S(1)} all-gather(bf16[1280,32]{0,1:T(8,128)(2,1)S(1)} %copy.7), channel_id=1, replica_groups=mesh['rows'=4,'slopes'=8] {'slopes'}, dimensions={1}, use_global_device_ids=true | all-gather | bytes 737280 | tf_op jit(solution)/shard_map/all_gather | solution.py:24
  55.9 0.9 dynamic-slice_select_fusion.1
  56.8 144.5 %all-gather.9.cloned.1.call-done = bf16[1280,5120]{1,0:T(8,128)(2,1)} async-done(((bf16[1280,640]{1,0:T(8,128)(2,1)}), bf16[1280,5120]{1,0:T(8,128)(2,1)}) %all-gather.9.cloned.1.call-update) | async-done | bytes 13107216 | tf_op jit(solution)/shard_map/all_gather | solution.py:23
  201.3 8.0 %dynamic-slice_select_fusion = bf16[640,5120]{1,0:T(8,128)(2,1)} fusion(bf16[1280,5120]{1,0:T(8,128)(2,1)} %all-gather.9.cloned.1.call-done, s32[]{:T(128)S(6)} %min.4, pred[]{:T(512)S(6)} %eq.4), kind=kLoop, calls=%fused_computation | loop fusion | flops 3276800 | bytes 13107205 | tf_op jit(solution)/shard_map/jit(_where)/select_n | solution.py:12
  209.2 0.0 all-reduce.4.cloned.1.call-update
  209.3 0.0 all-gather.7.cloned.1.call-start
  209.3 35.1 %all-gather.5.cloned.1.call-done = bf16[11264,256]{0,1:T(8,128)(2,1)} async-done(((bf16[11264,64]{0,1:T(8,128)(2,1)}), bf16[11264,256]{0,1:T(8,128)(2,1)}) %all-gather.5.cloned.1.call-update) | async-done | bytes 5767184 | tf_op jit(solution)/shard_map/all_gather | solution.py:28
  244.4 17.1 %fusion.3 = f32[1280,256]{1,0:T(8,128)} fusion(bf16[1280,11264]{1,0:T(8,128)(2,1)} %param.4, bf16[11264,256]{0,1:T(8,128)(2,1)} %all-gather.5.cloned.1.call-done), kind=kOutput, calls=%fused_computation.7 | convolution fusion | flops 7381975040 | bytes 35913728 | tf_op jit(solution)/shard_map/dot_general | solution.py:26
  261.5 76.8 %all-reduce.5 = bf16[1280,256]{1,0:T(8,128)(2,1)} all-reduce(f32[1280,256]{1,0:T(8,128)} %fusion.3), channel_id=1, replica_groups=mesh['rows'=4,'slopes'=8] {'slopes'}, use_global_device_ids=true, to_apply=%region_0.0 | all-reduce | flops 327680 | bytes 1966080 | tf_op jit(solution)/shard_map/psum | solution.py:31
  338.4 38.3 %all-reduce.4.cloned.1.call-done = (bf16[640,256]{0,1:T(8,128)(2,1)}, bf16[640,5120]{1,0:T(8,128)(2,1)}) async-done(((bf16[640,256]{0,1:T(8,128)(2,1)}, bf16[640,5120]{1,0:T(8,128)(2,1)}), (bf16[640,256]{0,1:T(8,128)(2,1)}, bf16[640,5120]{1,0:T(8,128)(2,1)})) %all-reduce.4.cloned.1.call-update) | async-done | bytes 6881296 | tf_op jit(solution)/shard_map/psum | solution.py:12
  376.7 4.1 fusion.2
  380.8 0.0 all-gather.7.cloned.1.call-update
  380.8 0.2 all-gather.11.cloned.1.call-start
  381.0 48.0 %all-gather.7.cloned.1.call-done = bf16[5120,640]{1,0:T(8,128)(2,1)} async-done(((bf16[1280,640]{1,0:T(8,128)(2,1)}), bf16[5120,640]{1,0:T(8,128)(2,1)}) %all-gather.7.cloned.1.call-update) | async-done | bytes 6553616 | tf_op jit(solution)/shard_map/all_gather | solution.py:45
  429.0 14.1 %fusion = bf16[1280,640]{0,1:T(8,128)(2,1)} fusion(bf16[5120,640]{1,0:T(8,128)(2,1)} %all-gather.7.cloned.1.call-done, bf16[1280,5120]{1,0:T(8,128)(2,1)} %all-gather.9.cloned.1.call-done), kind=kOutput, calls=%fused_computation.3 | convolution fusion | flops 8389427200 | bytes 21299200 | tf_op jit(solution)/shard_map/dot_general | solution.py:43
  443.1 182.6 %all-gather.11.cloned.1.call-done = bf16[1280,5120]{0,1:T(8,128)(2,1)} async-done(((bf16[1280,640]{0,1:T(8,128)(2,1)}), bf16[1280,5120]{0,1:T(8,128)(2,1)}) %all-gather.11.cloned.1.call-update) | async-done | bytes 13107216 | tf_op jit(solution)/shard_map/all_gather | solution.py:50
  625.8 16.5 %fusion.4 = f32[1280,640]{1,0:T(8,128)} fusion(bf16[1280,5120]{0,1:T(8,128)(2,1)} %all-gather.11.cloned.1.call-done, bf16[640,5120]{1,0:T(8,128)(2,1)} %get-tuple-element.3), kind=kOutput, calls=%fused_computation.8 | convolution fusion | flops 8388608000 | bytes 22937600 | tf_op jit(solution)/shard_map/dot_general | solution.py:49
  (3 shorter events, 0.0 us)
Async XLA Ops:
  7.2 194.1 %all-gather.9.cloned.1.call-start = ((), (), s32[]{:S(2)}) async-start(), calls=%async_computation.2 | async-start | bytes 14745600 | tf_op jit(solution)/shard_map/all_gather | solution.py:23
  7.9 236.5 %all-gather.5.cloned.1.call-start = ((), (), s32[]{:S(2)}) async-start(), calls=%async_computation | async-start | bytes 7208960 | tf_op jit(solution)/shard_map/all_gather | solution.py:28
  8.6 368.0 %all-reduce.4.cloned.1.call-start = ((), (), s32[]{:S(2)}) async-start(), calls=%async_computation.4 | async-start | bytes 13762560 | tf_op jit(solution)/shard_map/psum | solution.py:12
  209.3 167.4 %copy-start = (f32[1280,640]{1,0:T(8,128)S(1)}, f32[1280,640]{1,0:T(8,128)}, u32[]{:S(2)}) copy-start(f32[1280,640]{1,0:T(8,128)} %param.6) | copy-start | bytes 9830404
  209.3 219.7 %all-gather.7.cloned.1.call-start = ((), (), s32[]{:S(2)}) async-start(), calls=%async_computation.1 | async-start | bytes 8192000 | tf_op jit(solution)/shard_map/all_gather | solution.py:45
  380.8 245.0 %all-gather.11.cloned.1.call-start = ((), (), s32[]{:S(2)}) async-start(), calls=%async_computation.3 | async-start | bytes 14745600 | tf_op jit(solution)/shard_map/all_gather | solution.py:50
Sparse Core Ops, SparseCore 0:
  10.2 191.0 all-gather.8
  202.8 41.5 all-gather.4
  247.4 129.1 all-reduce.3
  380.9 48.0 all-gather.6
  443.2 182.4 all-gather.10
where the time goes:
time: 649 us
  waiting for transfers between devices  450 us (69%)
  blocking collectives  113 us (17%)
  matrix products  51.7 us (8%)
  between operations  13.8 us (2%)
  local copies, waits for them, and re-layouts  10.9 us (2%)
  other arithmetic  8.85 us (1%)
    all_gather x1, waiting for transfers between devices, body(): lax.all_gather(front, 'slopes', axis=1, tiled=True)  183 us
    all_gather x1, waiting for transfers between devices, body(): lax.all_gather(propagation, 'slopes', axis=1, tiled=True)  144 us
    psum x1, blocking collectives, body(): reach = lax.psum(partial_sum, 'slopes').astype(jnp.bfloat16)  76.8 us
    all_gather x1, waiting for transfers between devices, body(): lax.all_gather(resid_low, 'rows', axis=0, tiled=True)  48 us
    psum x1, waiting for transfers between devices, spread(): return lax.psum(jnp.where(mine, x, jnp.zeros_like(x)), axis)  38.3 us
    all_gather x1, blocking collectives, body(): lax.all_gather(picked_local, 'slopes', axis=1, tiled=True)  36.3 us
    all_gather x1, waiting for transfers between devices, body(): lax.all_gather(cov_slab, 'rows', axis=1, tiled=True)  35.1 us
    dot_general x1, matrix products, body(): jnp.dot(reconstructor, lax.all_gather(cov_slab, 'rows', axis=1, tiled=Tru...  17.1 us
  transfers between devices with their start and end apart: 5, of which 5 were waited for; matrix products, arithmetic and copies ran while one was open for 6% of the time, Pallas kernels for 0%

commit v1 on v0

--- a/solution.py
+++ b/solution.py
@@ -20,7 +20,10 @@
     stride = SLOPES // SLAB
     picked_local = reconstructor[:, ::stride]
     d_rows, picked_rows = (
-        lax.all_gather(propagation, "slopes", axis=1, tiled=True),
+        jnp.concatenate(
+            lax.all_to_all(jnp.stack([propagation] * lax.axis_size("slopes")), "slopes", 0, 0),
+            axis=1,
+        ),
         lax.all_gather(picked_local, "slopes", axis=1, tiled=True),
     )
     partial_sum = jnp.dot(

time: 649 us -> 741 us (1.14)
  blocking collectives: 113 us -> 369 us
  waiting for transfers between devices: 450 us -> 268 us
  local copies, waits for them, and re-layouts: 10.9 us -> 19.5 us
    all_gather x1, blocking collectives: 36.3 us -> 294 us  [body(): lax.all_gather(picked_local, 'slopes', axis=1, tiled=True)]
    all_gather x1 -> x0, waiting for transfers between devices: 144 us -> none  [body(): lax.all_gather(propagation, 'slopes', axis=1, tiled=True)]
    all_gather x1, waiting for transfers between devices: 35.1 us -> 0.02 us  [body(): lax.all_gather(cov_slab, 'rows', axis=1, tiled=True)]
  transfers between devices with their start and end apart: 5 -> 5, of which waited for: 5 -> 3; matrix products, arithmetic and copies ran while one was open for 6% -> 5% of each run, Pallas kernels for 0% -> 0%
where the time goes in v1:
time: 741 us
  blocking collectives  369 us (50%)
  waiting for transfers between devices  268 us (36%)
  matrix products  51.8 us (7%)
  local copies, waits for them, and re-layouts  19.5 us (3%)
  between operations  13.8 us (2%)
  other arithmetic  11.3 us (2%)
  starting transfers between devices  7.65 us (1%)
    all_gather x1, blocking collectives, body(): lax.all_gather(picked_local, 'slopes', axis=1, tiled=True)  294 us
    all_gather x1, waiting for transfers between devices, body(): lax.all_gather(front, 'slopes', axis=1, tiled=True)  183 us
    psum x1, blocking collectives, body(): reach = lax.psum(partial_sum, 'slopes').astype(jnp.bfloat16)  75.1 us
    all_gather x1, waiting for transfers between devices, body(): lax.all_gather(resid_low, 'rows', axis=0, tiled=True)  48 us
    psum x1, waiting for transfers between devices, spread(): return lax.psum(jnp.where(mine, x, jnp.zeros_like(x)), axis)  36.5 us
    dot_general x1, matrix products, body(): jnp.dot(reconstructor, lax.all_gather(cov_slab, 'rows', axis=1, tiled=Tru...  17 us
    dot_general x1, matrix products, body(): lax.dot_general(lax.all_gather(front, 'slopes', axis=1, tiled=True), colu...  16.5 us
  transfers between devices with their start and end apart: 5, of which 3 were waited for; matrix products, arithmetic and copies ran while one was open for 5% of the time, Pallas kernels for 0%

profile of v1, /device:TPU:0, one launch (start us, length us, event | category | flops | bytes accessed | tf_op | source)
XLA Modules:
  0.0 740.8 jit_solution(12986507380801744064)
XLA Ops:
  7.2 2.7 copy.8
  9.9 5.6 stack.2
  15.5 7.3 all-to-all-start
  22.8 0.0 all-gather.4.cloned.1.call-start
  22.8 0.7 all-gather.4.cloned.1.call-update
  23.5 0.0 all-reduce.4.cloned.1.call-start
  23.6 11.1 %slice.3 = bf16[1280,32]{1,0:T(8,128)(2,1)S(1)} slice(bf16[1280,11264]{1,0:T(8,128)(2,1)} %param.4), slice={[0:1280:1], [0:11264:352]} | slice | bytes 163840 | tf_op jit(solution)/shard_map/slice | solution.py:21
  34.7 0.2 copy.9
  34.8 293.7 %all_gather.13 = bf16[1280,256]{0,1:T(8,128)(2,1)S(1)} all-gather(bf16[1280,32]{0,1:T(8,128)(2,1)S(1)} %copy.9), channel_id=1, replica_groups=mesh['rows'=4,'slopes'=8] {'slopes'}, dimensions={1}, use_global_device_ids=true | all-gather | bytes 737280 | tf_op jit(solution)/shard_map/all_gather | solution.py:27
  328.5 0.9 dynamic-slice_select_fusion.1
  329.4 10.4 %dynamic-slice_select_fusion = bf16[640,5120]{0,1:T(8,128)(2,1)} fusion(bf16[1280,5120]{0,1:T(8,128)(2,1)} %bitcast.1, s32[]{:T(128)S(6)} %min.4, pred[]{:T(512)S(6)} %eq.4), kind=kLoop, calls=%fused_computation | loop fusion | flops 3276800 | bytes 13107205 | tf_op jit(solution)/shard_map/jit(_where)/select_n | solution.py:12
  339.8 0.0 all-reduce.4.cloned.1.call-update
  339.9 0.0 all-gather.6.cloned.1.call-start
  339.9 0.0 all-gather.4.cloned.1.call-done
  340.0 17.0 %fusion.3 = f32[1280,256]{1,0:T(8,128)} fusion(bf16[1280,11264]{1,0:T(8,128)(2,1)} %param.4, bf16[11264,256]{0,1:T(8,128)(2,1)} %all-gather.4.cloned.1.call-done), kind=kOutput, calls=%fused_computation.7 | convolution fusion | flops 7381975040 | bytes 35913728 | tf_op jit(solution)/shard_map/dot_general | solution.py:29
  357.0 75.1 %all-reduce.5 = bf16[1280,256]{1,0:T(8,128)(2,1)} all-reduce(f32[1280,256]{1,0:T(8,128)} %fusion.3), channel_id=1, replica_groups=mesh['rows'=4,'slopes'=8] {'slopes'}, use_global_device_ids=true, to_apply=%region_0.0 | all-reduce | flops 327680 | bytes 1966080 | tf_op jit(solution)/shard_map/psum | solution.py:34
  432.1 36.5 %all-reduce.4.cloned.1.call-done = (bf16[640,256]{0,1:T(8,128)(2,1)}, bf16[640,5120]{0,1:T(8,128)(2,1)}) async-done(((bf16[640,256]{0,1:T(8,128)(2,1)}, bf16[640,5120]{0,1:T(8,128)(2,1)}), (bf16[640,256]{0,1:T(8,128)(2,1)}, bf16[640,5120]{0,1:T(8,128)(2,1)})) %all-reduce.4.cloned.1.call-update) | async-done | bytes 6881296 | tf_op jit(solution)/shard_map/psum | solution.py:12
  468.5 4.1 fusion.2
  472.6 0.0 all-gather.6.cloned.1.call-update
  472.7 0.2 all-gather.8.cloned.1.call-start
  472.9 48.0 %all-gather.6.cloned.1.call-done = bf16[5120,640]{1,0:T(8,128)(2,1)} async-done(((bf16[1280,640]{1,0:T(8,128)(2,1)}), bf16[5120,640]{1,0:T(8,128)(2,1)}) %all-gather.6.cloned.1.call-update) | async-done | bytes 6553616 | tf_op jit(solution)/shard_map/all_gather | solution.py:48
  520.9 14.2 %fusion = bf16[1280,640]{0,1:T(8,128)(2,1)} fusion(bf16[5120,640]{1,0:T(8,128)(2,1)} %all-gather.6.cloned.1.call-done, bf16[1280,5120]{0,1:T(8,128)(2,1)} %bitcast.1), kind=kOutput, calls=%fused_computation.3 | convolution fusion | flops 8389427200 | bytes 21299200 | tf_op jit(solution)/shard_map/dot_general | solution.py:46
  535.1 182.6 %all-gather.8.cloned.1.call-done = bf16[1280,5120]{0,1:T(8,128)(2,1)} async-done(((bf16[1280,640]{0,1:T(8,128)(2,1)}), bf16[1280,5120]{0,1:T(8,128)(2,1)}) %all-gather.8.cloned.1.call-update) | async-done | bytes 13107216 | tf_op jit(solution)/shard_map/all_gather | solution.py:53
  717.7 16.5 %fusion.4 = f32[1280,640]{1,0:T(8,128)} fusion(bf16[1280,5120]{0,1:T(8,128)(2,1)} %all-gather.8.cloned.1.call-done, bf16[640,5120]{0,1:T(8,128)(2,1)} %get-tuple-element.3), kind=kOutput, calls=%fused_computation.8 | convolution fusion | flops 8388608000 | bytes 22937600 | tf_op jit(solution)/shard_map/dot_general | solution.py:52
  (4 shorter events, 0.0 us)
Async XLA Ops:
  15.5 314.0 %all-to-all-start = ((bf16[8,1280,640]{1,2,0:T(8,128)(2,1)}), bf16[8,1280,640]{1,2,0:T(8,128)(2,1)}, u32[]{:S(2)}, u32[]{:S(2)}) async-start(bf16[8,1280,640]{1,2,0:T(8,128)(2,1)} %stack.2), calls=%async_computation | async-start | bytes 26214400 | tf_op jit(solution)/shard_map/all_to_all | solution.py:24
  22.8 317.2 %all-gather.4.cloned.1.call-start = ((), (), s32[]{:S(2)}) async-start(), calls=%async_computation.1 | async-start | bytes 7208960 | tf_op jit(solution)/shard_map/all_gather | solution.py:31
  23.5 445.0 %all-reduce.4.cloned.1.call-start = ((), (), s32[]{:S(2)}) async-start(), calls=%async_computation.4 | async-start | bytes 13762560 | tf_op jit(solution)/shard_map/psum | solution.py:12
  339.9 128.7 %copy-start = (f32[1280,640]{1,0:T(8,128)S(1)}, f32[1280,640]{1,0:T(8,128)}, u32[]{:S(2)}) copy-start(f32[1280,640]{1,0:T(8,128)} %param.6) | copy-start | bytes 9830404
  339.9 181.0 %all-gather.6.cloned.1.call-start = ((), (), s32[]{:S(2)}) async-start(), calls=%async_computation.2 | async-start | bytes 8192000 | tf_op jit(solution)/shard_map/all_gather | solution.py:48
  472.7 245.1 %all-gather.8.cloned.1.call-start = ((), (), s32[]{:S(2)}) async-start(), calls=%async_computation.3 | async-start | bytes 14745600 | tf_op jit(solution)/shard_map/all_gather | solution.py:53
Sparse Core Ops, SparseCore 0:
  25.1 44.7 all-gather.3
  340.0 128.5 all-reduce.3
  472.8 48.0 all-gather.5
  535.2 182.4 all-gather.7
